TPU v7x, 256 devices: a whole 4x4x8 slice. The times are simulated.
256 devices in a mesh: tab: 64 (over x, z, core), rep: 4 (over y).
Axes of the slice: x: 4, y: 4, z: 8, core: 2. Of those that a mesh axis runs over, the one named last changes fastest.
Arguments:
- sample_ids: int32 [131072, 26], P(('tab', 'rep')), may hold values from 0 to 32767, as said below
- features: bfloat16 [131072, 27, 128], P(('tab', 'rep')), may hold values from -6 to 6
- pair_grad: bfloat16 [351, 131072], P(None, ('tab', 'rep')), may hold values from -1.59375 to 1.59375
Outputs:
- table_grad: float32 [26, 32768, 128], P(None, ('tab', 'rep'))
- dense_grad: float32 [131072, 128], P(('tab', 'rep'))
Inputs may be any that keep to these rules, and one draw needn't show every extreme that they name: `sample_ids`: row r is owned by device r // 128, numbered tab * 4 + rep. For each field and the 512 samples of one device (aligned blocks of rows in device order), at most 4 ids fall in the rows of any one device, and at most 16 in the rows of any one tab index; in every block and field both bounds are reached.
All inputs are finite; a program needn't handle non-finite values.
Results may differ from a plain program's by a relative error of at most 0.0029.
Values may be sent and summed in bfloat16 or wider, within the bound.
A program may use at most 128 MiB of HBM per device.

v0:
```python
import jax
import jax.numpy as jnp
import numpy as np
from jax import lax
from jax.sharding import PartitionSpec as P

RQ = 128


def pair_table(vectors):
    row_of, col_of = np.tril_indices(vectors, -1)
    spread = np.zeros((row_of.shape[0], vectors * vectors), np.float32)
    places = np.arange(row_of.shape[0])
    spread[places, row_of * vectors + col_of] = 1.0
    spread[places, col_of * vectors + row_of] = 1.0
    return spread


def arrival_order(targets, bins):
    matches = (targets[:, None] == jnp.arange(bins, dtype=jnp.int32)[None, :]).astype(jnp.int32)
    return jnp.sum(jnp.cumsum(matches, axis=0) * matches, axis=1) - 1


def place_field(slot_of, tag_of, grads, slot_total):
    placing = jnp.arange(slot_total, dtype=jnp.int32)[:, None] == slot_of[None, :]
    placed = jnp.dot(
        placing.astype(jnp.bfloat16), grads, preferred_element_type=jnp.float32
    ).astype(jnp.bfloat16)
    shifted = (tag_of + 1).astype(jnp.float32)
    tag_sum = jnp.dot(placing.astype(jnp.float32), shifted, precision=lax.Precision.HIGHEST)
    return (placed, tag_sum.astype(jnp.int32) - 1)


def tally_rows(arrived, row_tags, row_count):

    def per_field(pieces):
        slot_grads, slot_tags = pieces
        matches = (slot_tags[None, :] == jnp.arange(row_count, dtype=jnp.int32)[:, None]).astype(
            jnp.bfloat16
        )
        return jnp.dot(matches, slot_grads, preferred_element_type=jnp.float32)

    return lax.map(per_field, (arrived, row_tags))


def local(sample_ids, features, pair_grad):
    vectors = features.shape[1]
    samples = features.shape[0]
    depth = features.shape[2]
    spread = jnp.asarray(pair_table(vectors).T).astype(jnp.bfloat16)
    symmetric = jnp.dot(spread, pair_grad, preferred_element_type=jnp.float32)
    symmetric = symmetric.astype(jnp.bfloat16).reshape(vectors, vectors, samples)
    gradients = jnp.einsum("fgb,bge->fbe", symmetric, features, preferred_element_type=jnp.float32)
    dense_grad = gradients[0]
    field_grads = gradients[1:].astype(jnp.bfloat16)
    fields = vectors - 1
    col_count = lax.axis_size("tab")
    rep_count = lax.axis_size("rep")
    capacity = 2 * samples // (col_count * rep_count)
    slot_total = col_count * rep_count * capacity
    ids_by_field = sample_ids.T

    def build_owner(pieces):
        column_ids, grads = pieces
        owners = column_ids // RQ
        slot_of = owners * capacity + arrival_order(owners, col_count * rep_count)
        return place_field(slot_of, column_ids % RQ, grads, slot_total)

    outgoing, row_tags = lax.map(build_owner, (ids_by_field, field_grads))
    outgoing = outgoing.reshape(fields, col_count, rep_count, capacity, depth)
    row_tags = row_tags.reshape(fields, col_count, rep_count, capacity)
    arrived, tags_in = (
        lax.all_to_all(
            lax.all_to_all(outgoing, "tab", split_axis=1, concat_axis=1, tiled=True),
            "rep",
            split_axis=2,
            concat_axis=2,
            tiled=True,
        ),
        lax.all_to_all(
            lax.all_to_all(row_tags, "tab", split_axis=1, concat_axis=1, tiled=True),
            "rep",
            split_axis=2,
            concat_axis=2,
            tiled=True,
        ),
    )
    table_grad = tally_rows(arrived.reshape(fields, -1, depth), tags_in.reshape(fields, -1), RQ)
    return (table_grad, dense_grad)


def solution(mesh):
    placed = (P(("tab", "rep"), None), P(("tab", "rep"), None, None), P(None, ("tab", "rep")))
    return jax.shard_map(
        local,
        mesh=mesh,
        in_specs=placed,
        out_specs=(P(None, ("tab", "rep"), None), P(("tab", "rep"), None)),
        check_vma=False,
    )
```

profile of v0, /device:TPU:8, one launch (start us, length us, event | category | flops | bytes accessed | tf_op | source)
XLA Modules:
  0.0 522.2 jit_solution(6914962849379103909)
XLA Ops:
  0.7 2.7 convolution_convert_fusion
  3.4 2.2 reshape.112
  5.6 7.5 %copy.28 = bf16[27,27,512]{1,0,2:T(8,128)(2,1)} copy(bf16[27,27,512]{2,1,0:T(8,128)(2,1)} %reshape.112) | data formatting | bytes 1492992 | tf_op jit(solution)/shard_map/reshape | solution.py:52
  13.1 4.5 fusion.26
  18.8 2.1 copy-done.2
  20.9 3.1 copy.30
  24.0 142.8 %while.25 = (s32[]{:T(128)}, bf16[26,1024,128]{2,1,0:T(8,128)(2,1)}, s32[26,1024]{1,0:T(8,128)S(1)}, s32[26,512]{1,0:T(8,128)}, bf16[26,512,128]{2,1,0:T(8,128)(2,1)}, /*index=5*/s32[]{:T(128)}, s32[]{:T(128)}) while((s32[]{:T(128)}, bf16[26,1024,128]{2,1,0:T(8,128)(2,1)}, s32[26,1024]{1,0:T(8,128)S(1)}, s32[26,512]{1,0:T(8,128)}, ...), condition=%wide.region_4.5_spmd, body=%wide.region_0.4_spmd.sunk | while | flops 159154432 | bytes 3647589 | solution.py:69
  27.4 2.1 fusion.49
  32.9 2.1 fusion.49
  38.4 2.1 fusion.49
  43.9 2.1 fusion.49
  49.4 2.1 fusion.49
  54.9 2.1 fusion.49
  60.4 2.1 fusion.49
  65.9 2.1 fusion.49
  71.4 2.1 fusion.49
  76.9 2.1 fusion.49
  82.4 2.1 fusion.49
  87.9 2.1 fusion.49
  93.4 2.1 fusion.49
  98.8 2.1 fusion.49
  104.3 2.1 fusion.49
  109.8 2.1 fusion.49
  115.3 2.1 fusion.49
  120.8 2.1 fusion.49
  126.3 2.1 fusion.49
  131.8 2.1 fusion.49
  137.3 2.1 fusion.49
  142.8 2.1 fusion.49
  148.2 2.1 fusion.49
  153.7 2.1 fusion.49
  159.2 2.1 fusion.49
  164.7 2.1 fusion.49
  168.6 12.1 %all-to-all-start = ((s32[64,1,416]{2,1,0:T(1,128)}), s32[64,1,416]{2,1,0:T(1,128)S(1)}, u32[]{:S(2)}, u32[]{:S(2)}) async-start(s32[64,1,416]{2,1,0:T(1,128)} %reshape.119), calls=%async_computation | async-start | bytes 262144 | tf_op jit(solution)/shard_map/all_to_all | solution.py:81
  180.7 8.0 %copy.34 = bf16[26,64,4,4,128]{4,3,2,0,1:T(4,128)(2,1)} copy(bf16[26,64,4,4,128]{4,3,2,1,0:T(4,128)(2,1)} %bitcast.88) | data formatting | bytes 13631488 | tf_op jit(solution)/shard_map/reshape | solution.py:70
  188.8 2.0 all-to-all-done
  190.8 8.3 %all-to-all-start.2 = ((bf16[26,64,4,4,128]{4,3,2,0,1:T(4,128)(2,1)}), bf16[26,64,4,4,128]{4,3,2,0,1:T(4,128)(2,1)}, u32[]{:S(2)}, u32[]{:S(2)}) async-start(bf16[26,64,4,4,128]{4,3,2,0,1:T(4,128)(2,1)} %copy.34), calls=%async_computation.2 | async-start | bytes 13631488 | tf_op jit(solution)/shard_map/all_to_all | solution.py:74
  202.5 148.0 %all-to-all-done.2 = bf16[26,64,4,4,128]{4,3,2,0,1:T(4,128)(2,1)} async-done(((bf16[26,64,4,4,128]{4,3,2,0,1:T(4,128)(2,1)}), bf16[26,64,4,4,128]{4,3,2,0,1:T(4,128)(2,1)}, u32[]{:S(2)}, u32[]{:S(2)}) %all-to-all-start.2) | async-done | bytes 6815776 | tf_op jit(solution)/shard_map/all_to_all | solution.py:74
  350.5 4.9 all-to-all-start.1
  355.4 9.5 %copy.35 = bf16[26,64,4,4,128]{4,3,1,0,2:T(4,128)(2,1)} copy(bf16[26,64,4,4,128]{4,3,2,0,1:T(4,128)(2,1)} %all-to-all-done.2) | data formatting | bytes 13631488 | tf_op jit(solution)/shard_map/all_to_all | solution.py:74
  364.9 5.4 %all-to-all-start.3 = ((bf16[26,64,4,4,128]{4,3,1,0,2:T(4,128)(2,1)}), bf16[26,64,4,4,128]{4,3,1,0,2:T(4,128)(2,1)}, u32[]{:S(2)}, u32[]{:S(2)}) async-start(bf16[26,64,4,4,128]{4,3,1,0,2:T(4,128)(2,1)} %copy.35), calls=%async_computation.3 | async-start | bytes 13631488 | tf_op jit(solution)/shard_map/all_to_all | solution.py:73
  370.3 2.4 slice.26
  374.9 71.8 %all-to-all-done.3 = bf16[26,64,4,4,128]{4,3,1,0,2:T(4,128)(2,1)} async-done(((bf16[26,64,4,4,128]{4,3,1,0,2:T(4,128)(2,1)}), bf16[26,64,4,4,128]{4,3,1,0,2:T(4,128)(2,1)}, u32[]{:S(2)}, u32[]{:S(2)}) %all-to-all-start.3) | async-done | bytes 6815776 | tf_op jit(solution)/shard_map/all_to_all | solution.py:73
  446.8 8.8 %copy.36 = bf16[26,64,4,4,128]{4,3,2,1,0:T(4,128)(2,1)} copy(bf16[26,64,4,4,128]{4,3,1,0,2:T(4,128)(2,1)} %all-to-all-done.3) | data formatting | bytes 13631488 | tf_op jit(solution)/shard_map/all_to_all | solution.py:73
  455.6 66.7 %while.26 = (s32[]{:T(128)}, f32[26,128,128]{2,1,0:T(8,128)}, s32[26,1024]{1,0:T(8,128)}, bf16[26,1024,128]{2,1,0:T(8,128)(2,1)}, s32[]{:T(128)}) while((s32[]{:T(128)}, f32[26,128,128]{2,1,0:T(8,128)}, s32[26,1024]{1,0:T(8,128)}, bf16[26,1024,128]{2,1,0:T(8,128)(2,1)}, s32[]{:T(128)}) %tuple.62), condition=%wide.region_6.7_spmd, body=%wide.region_5.6_spmd.sunk | while | flops 33685504 | bytes 341065 | solution.py:43
  456.3 1.8 fusion.52
  458.9 1.8 fusion.52
  461.5 1.8 fusion.52
  464.0 1.8 fusion.52
  466.6 1.8 fusion.52
  469.2 1.8 fusion.52
  471.7 1.8 fusion.52
  474.3 1.8 fusion.52
  476.8 1.8 fusion.52
  479.4 1.8 fusion.52
  482.0 1.8 fusion.52
  484.5 1.8 fusion.52
  494.8 1.8 fusion.52
  497.4 1.8 fusion.52
  499.9 1.8 fusion.52
  505.1 1.8 fusion.52
  515.3 1.8 fusion.52
  517.9 1.8 fusion.52
  520.4 1.8 fusion.52
  (498 shorter events, 128.0 us)
Async XLA Ops:
  0.6 12.5 %copy-start = (bf16[512,27,128]{2,0,1:T(8,128)(2,1)S(1)}, bf16[512,27,128]{2,0,1:T(8,128)(2,1)}, u32[]{:S(2)}) copy-start(bf16[512,27,128]{2,0,1:T(8,128)(2,1)} %param.9) | copy-start | bytes 10616836
  17.7 3.2 copy-start.2
  20.9 3.1 copy-start.3
  168.6 22.2 %all-to-all-start = ((s32[64,1,416]{2,1,0:T(1,128)}), s32[64,1,416]{2,1,0:T(1,128)S(1)}, u32[]{:S(2)}, u32[]{:S(2)}) async-start(s32[64,1,416]{2,1,0:T(1,128)} %reshape.119), calls=%async_computation | async-start | bytes 262144 | tf_op jit(solution)/shard_map/all_to_all | solution.py:81
  190.8 159.6 %all-to-all-start.2 = ((bf16[26,64,4,4,128]{4,3,2,0,1:T(4,128)(2,1)}), bf16[26,64,4,4,128]{4,3,2,0,1:T(4,128)(2,1)}, u32[]{:S(2)}, u32[]{:S(2)}) async-start(bf16[26,64,4,4,128]{4,3,2,0,1:T(4,128)(2,1)} %copy.34), calls=%async_computation.2 | async-start | bytes 13631488 | tf_op jit(solution)/shard_map/all_to_all | solution.py:74
  350.5 14.5 %all-to-all-start.1 = ((s32[4,1,6656]{2,1,0:T(1,128)}), s32[4,1,6656]{2,1,0:T(1,128)S(1)}, u32[]{:S(2)}, u32[]{:S(2)}) async-start(s32[4,1,6656]{2,1,0:T(1,128)} %reshape.121), calls=%async_computation.1 | async-start | bytes 212992 | tf_op jit(solution)/shard_map/all_to_all | solution.py:80
  364.9 81.8 %all-to-all-start.3 = ((bf16[26,64,4,4,128]{4,3,1,0,2:T(4,128)(2,1)}), bf16[26,64,4,4,128]{4,3,1,0,2:T(4,128)(2,1)}, u32[]{:S(2)}, u32[]{:S(2)}) async-start(bf16[26,64,4,4,128]{4,3,1,0,2:T(4,128)(2,1)} %copy.35), calls=%async_computation.3 | async-start | bytes 13631488 | tf_op jit(solution)/shard_map/all_to_all | solution.py:73
  446.7 75.5 %copy-start.1 = (bf16[512,27,128]{2,0,1:T(8,128)(2,1)S(1)}, bf16[512,27,128]{2,0,1:T(8,128)(2,1)}, u32[]{:S(2)}) copy-start(bf16[512,27,128]{2,0,1:T(8,128)(2,1)} %param.9) | copy-start | bytes 10616836
where the time goes:
time: 530 us; the launch traced here: 522 us
  waiting for transfers between devices  222 us (42%)
  matrix products  135 us (25%)
  local copies, waits for them, and re-layouts  97.7 us (18%)
  other arithmetic  35.2 us (7%)
  starting transfers between devices  30.7 us (6%)
    all_to_all x1, waiting for transfers between devices, local(): lax.all_to_all(outgoing, 'tab', split_axis=1, concat_axis=1, tiled=True)  148 us
    all_to_all x1, waiting for transfers between devices, local(): lax.all_to_all(lax.all_to_all(outgoing, 'tab', split_axis=1, concat_axis=...  71.8 us
    dot_general x26, matrix products, place_field(): jnp.dot(placing.astype(jnp.bfloat16), grads, preferred_element_type=jnp.f...  54.4 us
    dot_general x26, matrix products, per_field(): return jnp.dot(matches, slot_grads, preferred_element_type=jnp.float32)  46.8 us
    dot_general x26, matrix products, place_field(): jnp.dot(placing.astype(jnp.float32), shifted, precision=lax.Precision.HIG...  26.3 us
    dynamic_slice x26, local copies, waits for them, and re-layouts, tally_rows(): return lax.map(per_field, (arrived, row_tags))  19.9 us
    add x26, other arithmetic, build_owner(): slot_of = owners * capacity + arrival_order(owners, col_count * rep_count)  19.3 us
    dynamic_slice x26, local copies, waits for them, and re-layouts, local(): outgoing, row_tags = lax.map(build_owner, (ids_by_field, field_grads))  18.8 us
  transfers between devices with their start and end apart: 4, of which 3 were waited for; matrix products, arithmetic and copies ran while one was open for 5% of the time, Pallas kernels for 0%

commit v1 on v0

v1 whole, which is shorter than its diff:
```python
import functools

import jax
import jax.numpy as jnp
import numpy as np
from jax import lax
from jax.experimental import pallas as pl
from jax.experimental.pallas import tpu as pltpu
from jax.sharding import PartitionSpec as P

RQ = 128
CAP = 4
B = 512
F = 26
E = 128
NZ = 8
NG = 32
GS = NZ * CAP
SLOTS = NG * GS
FC = 2
C = F // FC
AHEAD = 4
QUADS = 7
MESH = pl.DeviceIdType.MESH
BF = jnp.bfloat16
F32 = jnp.float32


def pair_table(vectors):
    row_of, col_of = np.tril_indices(vectors, -1)
    spread = np.zeros((row_of.shape[0], vectors * vectors), np.float32)
    places = np.arange(row_of.shape[0])
    spread[places, row_of * vectors + col_of] = 1.0
    spread[places, col_of * vectors + row_of] = 1.0
    return spread


def device_of(group, z):
    x, core, y = group // 8, (group // 4) % 2, group % 4
    return ((x * NZ + z) * 2 + core, y)


def iota(shape, dim):
    return lax.broadcasted_iota(jnp.int32, shape, dim)


def exchange_kernel(
    ids_ref, ids_t_ref, grads_hbm, out_ref,
    grads, slot_rows, slot_cols, tag_send, tag_recv, wanted, send, recv, part, rows_f32, ring,
    load_sem, send_sem, recv_sem, tag_send_sem, tag_recv_sem, ring_send_sem, ring_recv_sem,
):
    tab = lax.axis_index("tab")
    y = lax.axis_index("rep")
    x, z, core = tab // (NZ * 2), (tab // 2) % NZ, tab % 2
    me = (x * 2 + core) * 4 + y

    barrier = pltpu.get_barrier_semaphore()
    up = device_of(me, lax.rem(z + 1, NZ))
    down = device_of(me, lax.rem(z + NZ - 1, NZ))

    @pl.loop(1, NG)
    def _(i):
        pl.semaphore_signal(barrier, inc=1, device_id=device_of(lax.rem(me + i, NG), z), device_id_type=MESH)

    pl.semaphore_signal(barrier, inc=1, device_id=up, device_id_type=MESH)
    pl.semaphore_signal(barrier, inc=1, device_id=down, device_id_type=MESH)

    load = pltpu.make_async_copy(grads_hbm, grads, load_sem)
    load.start()

    slot_rows[...] = jnp.zeros(slot_rows.shape, F32)

    @pl.loop(0, QUADS)
    def _(quad):
        shifted = pltpu.roll(ids_ref[...], lax.rem(128 - 4 * quad, 128), 1)
        for q in range(4):
            field = quad * 4 + q
            own_c = shifted[:, q : q + 1] >> 7
            own_r = ids_t_ref[pl.ds(field, 1), :] >> 7
            pieces = []
            for block in range(B // 128):
                lanes = own_r[:, block * 128 : (block + 1) * 128]
                total = jnp.zeros((1, 128), F32)
                for other in range(block + 1):
                    same = own_c[other * 128 : (other + 1) * 128] == lanes
                    if other == block:
                        same = same & (iota((128, 128), 0) < iota((128, 128), 1))
                    total = total + jnp.sum(jnp.where(same, 1.0, 0.0), axis=0, keepdims=True)
                pieces.append(total)
            rank = jnp.concatenate(pieces, axis=1).astype(jnp.int32)
            group = ((own_r >> 6) << 3) | (own_r & 7)
            slot = group * GS + ((own_r >> 3) & 7) * CAP + rank
            slot_rows[pl.ds(field, 1), :] = slot.astype(F32)

    slot_cols[...] = slot_rows[...].T.astype(jnp.int32)

    @pl.loop(0, QUADS)
    def _(quad):
        back = lax.rem(128 - 4 * quad, 128)
        ids = pltpu.roll(ids_ref[...], back, 1)
        slots = pltpu.roll(slot_cols[...], back, 1)
        total = jnp.zeros((NG, 128), F32)
        for q in range(4):
            tag = ((ids[:, q : q + 1] & (RQ - 1)) + 1).astype(F32)
            place = (slots[:, q : q + 1] & (GS - 1)) + q * GS
            right = jnp.where(iota((B, 128), 1) == place, tag, 0.0).astype(BF)
            row = slot_rows[pl.ds(quad * 4 + q, 1), :].astype(jnp.int32)
            left = jnp.where(iota((NG, B), 0) == (row >> 5), 1.0, 0.0).astype(BF)
            total = total + jnp.dot(left, right, preferred_element_type=F32)
        tag_send[pl.ds(quad, NG, stride=8), :] = total

    tag_send[pl.ds(QUADS, NG, stride=8), :] = jnp.zeros((NG, 128), F32)
    pl.semaphore_wait(barrier, NG + 1)

    def rows8(g):
        return pl.ds(pl.multiple_of(g * 8, 8), 8)

    @pl.loop(1, NG)
    def _(i):
        g = lax.rem(me + i, NG)
        pltpu.make_async_remote_copy(
            src_ref=tag_send.at[rows8(g)], dst_ref=tag_recv.at[rows8(me)],
            send_sem=tag_send_sem, recv_sem=tag_recv_sem, device_id=device_of(g, z), device_id_type=MESH,
        ).start()

    pltpu.make_async_copy(tag_send.at[rows8(me)], tag_recv.at[rows8(me)], tag_recv_sem).start()
    load.wait()

    def place(chunk):
        @pl.loop(0, FC)
        def _(k):
            field = chunk * FC + k
            row = slot_rows[pl.ds(field, 1), :].astype(jnp.int32)
            data = grads[field]
            half = SLOTS // 2
            for h in range(2):
                hit = iota((half, B), 0) + h * half == row
                placed = jnp.dot(jnp.where(hit, 1.0, 0.0).astype(BF), data, preferred_element_type=F32)
                send[chunk, pl.ds(h * NG // 2, NG // 2), pl.ds(pl.multiple_of(k * GS, GS), GS), :] = (
                    placed.astype(BF).reshape(NG // 2, GS, E)
                )

        pltpu.make_async_copy(send.at[chunk, me], recv.at[chunk, me], recv_sem.at[chunk]).start()

        @pl.loop(1, NG)
        def _(i):
            g = lax.rem(me + i, NG)
            pltpu.make_async_remote_copy(
                src_ref=send.at[chunk, g], dst_ref=recv.at[chunk, me],
                send_sem=send_sem, recv_sem=recv_sem.at[chunk], device_id=device_of(g, z), device_id_type=MESH,
            ).start()

    @pl.loop(0, AHEAD)
    def _(chunk):
        place(chunk)

    pltpu.make_async_copy(tag_recv, tag_recv, tag_recv_sem).wait()
    tags = tag_recv[...].astype(BF)
    for q in range(4):
        col = iota((128, SLOTS), 1)
        spread = jnp.where(iota((128, SLOTS), 0) == q * GS + (col >> 9) * 16 + (col & 15), 1.0, 0.0).astype(BF)
        wide = jnp.dot(tags, spread, preferred_element_type=F32).reshape(NG, 8, SLOTS)
        source = (iota((NG, 8, SLOTS), 2) & 511) >> 4
        tag = jnp.sum(jnp.where(iota((NG, 8, SLOTS), 0) == source, wide, 0.0), axis=0).astype(jnp.int32)
        row = ((iota((8, SLOTS), 1) & 15) >> 2) * RQ + tag - 1
        wanted[q] = jnp.where(tag > 0, row, -1)

    def tally(chunk):
        pltpu.make_async_copy(recv.at[chunk], recv.at[chunk], recv_sem.at[chunk]).wait()

        @pl.loop(0, FC)
        def _(k):
            field = chunk * FC + k
            want = wanted[field % 4, pl.ds(field // 4, 1), :]
            for h in range(2):
                data = recv[chunk, :, pl.ds(pl.multiple_of(k * GS + h * 16, 16), 16), :].reshape(NG * 16, E)
                hit = iota((4 * RQ, NG * 16), 0) == want[:, h * 512 : (h + 1) * 512]
                rows = jnp.dot(jnp.where(hit, 1.0, 0.0).astype(BF), data, preferred_element_type=F32)
                rows_f32[pl.ds(h * 4 * RQ, 4 * RQ), :] = rows
                part[chunk, pl.ds(h * 4, 4), pl.ds(pl.multiple_of(k * RQ, RQ), RQ), :] = rows.astype(BF).reshape(4, RQ, E)
            out_ref[field] = rows_f32[pl.ds(pl.multiple_of(z * RQ, RQ), RQ), :]

    def owner(d, step):
        away = 4 - step
        return lax.rem(z + (away if d == 0 else NZ - away), NZ)

    def arrived(d, step, chunk):
        size = FC * RQ if step else RQ
        ref = ring.at[d, step, chunk, pl.ds(0, size)]
        pltpu.make_async_copy(ref, ref, ring_recv_sem.at[d, step, chunk]).wait()

    def add(step, chunk):
        for d in range(2):
            arrived(d, step - 1, chunk)
            o = owner(d, step)
            if step == 1:
                part[chunk, o, pl.ds(d * RQ, RQ), :] = (
                    part[chunk, o, pl.ds(d * RQ, RQ), :].astype(F32) + ring[d, 0, chunk, pl.ds(0, RQ), :].astype(F32)
                ).astype(BF)
            else:
                part[chunk, o] = (part[chunk, o].astype(F32) + ring[d, step - 1, chunk].astype(F32)).astype(BF)

    def forward(step, chunk):
        for d in range(2):
            o = owner(d, step)
            src = part.at[chunk, o, pl.ds(d * RQ, RQ)] if step == 0 else part.at[chunk, o]
            dst = ring.at[d, 0, chunk, pl.ds(0, RQ)] if step == 0 else ring.at[d, step, chunk]
            pltpu.make_async_remote_copy(
                src_ref=src, dst_ref=dst, send_sem=ring_send_sem.at[d], recv_sem=ring_recv_sem.at[d, step, chunk],
                device_id=up if d == 0 else down, device_id_type=MESH,
            ).start()

    def finish(chunk):
        for d in range(2):
            arrived(d, 3, chunk)
        both = ring[0, 3, chunk].astype(F32) + ring[1, 3, chunk].astype(F32)
        for k in range(FC):
            out_ref[chunk * FC + k] += both[k * RQ : (k + 1) * RQ]

    @pl.loop(0, C + 4)
    def _(t):
        @pl.when(t + AHEAD < C)
        def _():
            place(t + AHEAD)

        @pl.when(t < C)
        def _():
            tally(t)

        for step in range(1, 4):

            @pl.when((t >= step) & (t < C + step))
            def _():
                add(step, t - step)

        @pl.when(t >= 4)
        def _():
            finish(t - 4)

        for step in range(4):

            @pl.when((t >= step) & (t < C + step))
            def _():
                forward(step, t - step)

    sent = send.at[:, pl.ds(0, NG - 1)]
    pltpu.make_async_copy(sent, sent, send_sem).wait()
    tags_sent = tag_send.at[pl.ds(0, (NG - 1) * 8)]
    pltpu.make_async_copy(tags_sent, tags_sent, tag_send_sem).wait()
    for d in range(2):
        for step in range(4):
            ref = ring.at[d, step, :, pl.ds(0, FC * RQ if step else RQ)]
            pltpu.make_async_copy(ref, ref, ring_send_sem.at[d]).wait()


def exchange(ids, ids_t, grads):
    vmem = pl.BlockSpec(memory_space=pltpu.VMEM)
    dma = pltpu.SemaphoreType.DMA
    return pl.pallas_call(
        exchange_kernel,
        out_shape=jax.ShapeDtypeStruct((F, RQ, E), F32),
        in_specs=[vmem, vmem, pl.BlockSpec(memory_space=pl.ANY)],
        out_specs=vmem,
        scratch_shapes=[
            pltpu.VMEM((F, B, E), BF),
            pltpu.VMEM((128, B), F32),
            pltpu.VMEM((B, 128), jnp.int32),
            pltpu.VMEM((NG * 8, 128), F32),
            pltpu.VMEM((NG * 8, 128), F32),
            pltpu.VMEM((4, 8, SLOTS), jnp.int32),
            pltpu.VMEM((C, NG, FC * GS, E), BF),
            pltpu.VMEM((C, NG, FC * GS, E), BF),
            pltpu.VMEM((C, NZ, FC * RQ, E), BF),
            pltpu.VMEM((NZ * RQ, E), F32),
            pltpu.VMEM((2, 4, C, FC * RQ, E), BF),
            dma, dma, dma((C,)), dma, dma, dma((2,)), dma((2, 4, C)),
        ],
        compiler_params=pltpu.CompilerParams(
            collective_id=0, has_side_effects=True, vmem_limit_bytes=60 * 2**20
        ),
        name="exchange",
    )(ids, ids_t, grads)


def local(sample_ids, features, pair_grad):
    vectors = features.shape[1]
    samples = features.shape[0]
    spread = jnp.asarray(pair_table(vectors).T).astype(BF)
    symmetric = jnp.dot(spread, pair_grad, preferred_element_type=F32)
    symmetric = symmetric.astype(BF).reshape(vectors, vectors, samples)
    gradients = jnp.einsum("fgb,bge->fbe", symmetric, features, preferred_element_type=F32)
    dense_grad = gradients[0]
    field_grads = gradients[1:].astype(BF)
    ids = jnp.pad(sample_ids, ((0, 0), (0, 128 - F)))
    ids_t = jnp.pad(sample_ids.T, ((0, 32 - F), (0, 0)))
    return (exchange(ids, ids_t, field_grads), dense_grad)


def solution(mesh):
    placed = (P(("tab", "rep"), None), P(("tab", "rep"), None, None), P(None, ("tab", "rep")))
    return jax.shard_map(
        local,
        mesh=mesh,
        in_specs=placed,
        out_specs=(P(None, ("tab", "rep"), None), P(("tab", "rep"), None)),
        check_vma=False,
    )
```

time: 530 us -> 172 us (0.32); the launches traced: 522 us -> 170 us
  waiting for transfers between devices: 222 us -> 0 us
  Pallas kernels: 0 us -> 133 us
  matrix products: 135 us -> 7.27 us
  local copies, waits for them, and re-layouts: 97.7 us -> 28.4 us
  other arithmetic: 35.2 us -> 0 us
  starting transfers between devices: 30.7 us -> 0 us
    all_to_all x4 -> x0, waiting for transfers between devices: 222 us -> none  [the longest x1 148 us: local(): lax.all_to_all(outgoing, 'tab', split_axis=1, concat_axis=1, tiled=True)]
    pallas_call x0 -> x1, Pallas kernels: none -> 133 us  [exchange(): pl.pallas_call(exchange_kernel, out_shape=jax.ShapeDtypeStruct((F, RQ, E)...]
    dot_general x80 -> x2, matrix products: 135 us -> 7.27 us  [the longest x1 4.54 us: local(): jnp.einsum('fgb,bge->fbe', symmetric, features, preferred_element_type=F32)]
    dynamic_slice x52 -> x0, local copies, waits for them, and re-layouts: 38.6 us -> none  [the longest x26 19.9 us: tally_rows(): return lax.map(per_field, (arrived, row_tags))]
    all_to_all x4 -> x0, starting transfers between devices: 30.7 us -> none  [the longest x1 12.1 us: local(): lax.all_to_all(row_tags, 'tab', split_axis=1, concat_axis=1, tiled=True)]
    all_to_all x5 -> x0, local copies, waits for them, and re-layouts: 19.6 us -> none  [the longest x1 9.53 us: local(): lax.all_to_all(outgoing, 'tab', split_axis=1, concat_axis=1, tiled=True)]
    add x26 -> x0, other arithmetic: 19.3 us -> none  [build_owner(): slot_of = owners * capacity + arrival_order(owners, col_count * rep_count)]
    reshape x3 -> x2, local copies, waits for them, and re-layouts: 17.8 us -> 9.73 us  [local(): symmetric = symmetric.astype(BF).reshape(vectors, vectors, samples)]
  transfers between devices with their start and end apart: 4 -> 0, of which waited for: 3 -> 0; matrix products, arithmetic and copies ran while one was open for 5% -> 0% of each run, Pallas kernels for 0% -> 0%
where the time goes in v1:
time: 172 us; the launch traced here: 170 us
  Pallas kernels  133 us (77%)
  local copies, waits for them, and re-layouts  28.4 us (17%)
  matrix products  7.27 us (4%)
    pallas_call x1, Pallas kernels, exchange(): pl.pallas_call(exchange_kernel, out_shape=jax.ShapeDtypeStruct((F, RQ, E)...  133 us
    reshape x2, local copies, waits for them, and re-layouts, local(): symmetric = symmetric.astype(BF).reshape(vectors, vectors, samples)  9.73 us
    unnamed x6, local copies, waits for them, and re-layouts  7.42 us
    dot_general x1, matrix products, local(): jnp.einsum('fgb,bge->fbe', symmetric, features, preferred_element_type=F32)  4.54 us
    dot_general x1, local copies, waits for them, and re-layouts, local(): jnp.einsum('fgb,bge->fbe', symmetric, features, preferred_element_type=F32)  4.1 us

profile of v1, /device:TPU:8, one launch (start us, length us, event | category | flops | bytes accessed | tf_op | source)
XLA Modules:
  0.0 169.6 jit_solution(9633527800407476824)
XLA Ops:
  0.6 0.0 copy-start
  0.6 2.7 %convolution_convert_fusion = bf16[729,512]{1,0:T(8,128)(2,1)} fusion(bf16[729,351]{1,0:T(8,128)(2,1)} %constant.9, bf16[351,512]{1,0:T(8,128)(2,1)} %param.6), kind=kOutput, calls=%fused_computation.4 | convolution fusion | flops 262393344 | bytes 1617678 | tf_op jit(solution)/shard_map/dot_general | solution.py:289
  3.4 2.2 %reshape.7 = bf16[27,27,512]{2,1,0:T(8,128)(2,1)} reshape(bf16[729,512]{1,0:T(8,128)(2,1)} %convolution_convert_fusion) | data formatting | bytes 1492992 | tf_op jit(solution)/shard_map/reshape | solution.py:290
  5.6 7.5 %copy.7 = bf16[27,27,512]{1,0,2:T(8,128)(2,1)} copy(bf16[27,27,512]{2,1,0:T(8,128)(2,1)} %reshape.7) | data formatting | bytes 1492992 | tf_op jit(solution)/shard_map/reshape | solution.py:290
  13.1 0.0 copy-done
  13.1 4.5 %fusion = f32[512,27,128]{2,1,0:T(8,128)S(1)} fusion(bf16[27,27,512]{1,0,2:T(8,128)(2,1)} %copy.7, bf16[512,27,128]{2,0,1:T(8,128)(2,1)S(1)} %copy-done), kind=kOutput, calls=%fused_computation.2 | convolution fusion | flops 95551488 | bytes 11363328 | tf_op jit(solution)/shard_map/fgb,bge->fbe/dot_general | solution.py:291
  17.6 4.1 %copy.13 = f32[512,27,128]{2,0,1:T(8,128)S(1)} copy(f32[512,27,128]{2,1,0:T(8,128)S(1)} %fusion) | data formatting | bytes 14155776 | tf_op jit(solution)/shard_map/fgb,bge->fbe/dot_general | solution.py:291
  21.7 0.0 copy-start.1
  21.8 2.9 %copy-done.1 = f32[512,27,128]{2,0,1:T(8,128)} copy-done((f32[512,27,128]{2,0,1:T(8,128)}, f32[512,27,128]{2,0,1:T(8,128)S(1)}, u32[]{:S(2)}) %copy-start.1) | copy-done | bytes 7077912
  24.7 2.4 %slice.13.grads_hbm = bf16[26,512,128]{2,1,0:T(8,128)(2,1)} slice(f32[27,512,128]{2,1,0:T(8,128)S(1)} %bitcast.9), slice={[1:27], [0:512], [0:128]} | slice | bytes 6815744 | tf_op jit(solution)/shard_map/slice | solution.py:293
  27.0 1.7 copy.6
  28.7 1.7 pad.8.ids_ref
  30.4 1.5 pad.9.ids_t_ref
  31.9 133.3 %exchange.1 = f32[26,128,128]{2,1,0:T(8,128)} custom-call(s32[512,128]{1,0:T(8,128)} %pad.8.ids_ref, s32[32,512]{1,0:T(8,128)} %pad.9.ids_t_ref, bf16[26,512,128]{2,1,0:T(8,128)(2,1)} %slice.13.grads_hbm), custom_call_target="tpu_custom_call" | custom-call | tf_op jit(solution)/shard_map/exchange/pallas_call | solution.py:259
  165.1 1.7 slice_bitcast_fusion
  166.8 2.8 %copy.15 = f32[26,128,128]{2,1,0:T(8,128)} copy(f32[26,128,128]{2,1,0:T(8,128)} %exchange.1) | data formatting | bytes 3407872
Async XLA Ops:
  0.6 12.5 %copy-start = (bf16[512,27,128]{2,0,1:T(8,128)(2,1)S(1)}, bf16[512,27,128]{2,0,1:T(8,128)(2,1)}, u32[]{:S(2)}) copy-start(bf16[512,27,128]{2,0,1:T(8,128)(2,1)} %param.5) | copy-start | bytes 10616836
  21.7 2.9 %copy-start.1 = (f32[512,27,128]{2,0,1:T(8,128)}, f32[512,27,128]{2,0,1:T(8,128)S(1)}, u32[]{:S(2)}) copy-start(f32[512,27,128]{2,0,1:T(8,128)S(1)} %copy.13) | copy-start | bytes 21233668

commit v2 on v1

--- a/solution.py
+++ b/solution.py
@@ -26,12 +26,18 @@
 F32 = jnp.float32
 
 
-def pair_table(vectors):
-    row_of, col_of = np.tril_indices(vectors, -1)
-    spread = np.zeros((row_of.shape[0], vectors * vectors), np.float32)
-    places = np.arange(row_of.shape[0])
-    spread[places, row_of * vectors + col_of] = 1.0
-    spread[places, col_of * vectors + row_of] = 1.0
+V = F + 1
+PAIRS = V * F // 2
+SB = 16
+NB = B // SB
+
+
+def pair_table():
+    row_of, col_of = np.tril_indices(V, -1)
+    spread = np.zeros((384, QUADS * 128), np.float32)
+    places = np.arange(PAIRS)
+    spread[places, row_of * 32 + col_of] = 1.0
+    spread[places, col_of * 32 + row_of] = 1.0
     return spread
 
 
@@ -45,8 +51,8 @@
 
 
 def exchange_kernel(
-    ids_ref, ids_t_ref, grads_hbm, out_ref,
-    grads, slot_rows, slot_cols, tag_send, tag_recv, wanted, send, recv, part, rows_f32, ring,
+    ids_ref, feats_hbm, pairs_ref, table_ref, out_ref, dense_ref,
+    feats, pairs, picked, expand, left, grads, ids_rows, ids_cols, slot_rows, slot_cols, tag_send, tag_recv, wanted, send, recv, part, rows_f32, ring,
     load_sem, send_sem, recv_sem, tag_send_sem, tag_recv_sem, ring_send_sem, ring_recv_sem,
 ):
     tab = lax.axis_index("tab")
@@ -65,18 +71,51 @@
     pl.semaphore_signal(barrier, inc=1, device_id=up, device_id_type=MESH)
     pl.semaphore_signal(barrier, inc=1, device_id=down, device_id_type=MESH)
 
-    load = pltpu.make_async_copy(grads_hbm, grads, load_sem)
+    load = pltpu.make_async_copy(feats_hbm, feats, load_sem)
     load.start()
 
-    slot_rows[...] = jnp.zeros(slot_rows.shape, F32)
+    pairs[...] = jnp.zeros(pairs.shape, F32)
+    pairs[pl.ds(0, PAIRS), :] = pairs_ref[...].astype(F32)
+    by_sample = pairs[...].T.astype(BF)
+    for quad in range(QUADS):
+        picked[quad] = jnp.dot(
+            by_sample, table_ref[:, quad * 128 : (quad + 1) * 128], preferred_element_type=F32
+        ).astype(BF)
+    for q in range(4):
+        expand[q] = jnp.where(
+            iota((128, 32 * SB), 0) == q * 32 + (iota((128, 32 * SB), 1) >> 4), 1.0, 0.0
+        ).astype(BF)
 
     @pl.loop(0, QUADS)
     def _(quad):
-        shifted = pltpu.roll(ids_ref[...], lax.rem(128 - 4 * quad, 128), 1)
+        @pl.loop(0, 4)
+        def _(q):
+            wide = jnp.dot(picked[quad], expand[q], preferred_element_type=F32).reshape(NB, SB, 32 * SB)
+            own = iota((1, SB, 32 * SB), 1) == (iota((1, SB, 32 * SB), 2) & (SB - 1))
+            left[:, pl.ds(pl.multiple_of((quad * 4 + q) * SB, SB), SB), :] = jnp.where(own, wide, 0.0).astype(BF)
+
+    load.wait()
+
+    @pl.loop(0, NB)
+    def _(g):
+        at = pl.ds(pl.multiple_of(g * SB, SB), SB)
+        right = jnp.concatenate([feats[:, at, :], jnp.zeros((32 - V, SB, E), BF)], axis=0).reshape(32 * SB, E)
+        result = jnp.dot(left[g], right, preferred_element_type=F32).reshape(4 * QUADS, SB, E)
+        dense_ref[at, :] = result[0]
+        grads[:, at, :] = result[1:V].astype(BF)
+
+    ids_rows[...] = jnp.zeros(ids_rows.shape, F32)
+    ids_rows[pl.ds(0, F), :] = ids_ref[...].astype(F32)
+    ids_cols[...] = ids_rows[...].T.astype(jnp.int32)
+
+    slot_rows[...] = jnp.zeros(slot_rows.shape, F32)
+
+    def rank_quad(quad):
+        shifted = pltpu.roll(ids_cols[...], lax.rem(128 - 4 * quad, 128), 1)
         for q in range(4):
             field = quad * 4 + q
             own_c = shifted[:, q : q + 1] >> 7
-            own_r = ids_t_ref[pl.ds(field, 1), :] >> 7
+            own_r = ids_rows[pl.ds(field, 1), :].astype(jnp.int32) >> 7
             pieces = []
             for block in range(B // 128):
                 lanes = own_r[:, block * 128 : (block + 1) * 128]
@@ -92,40 +131,6 @@
             slot = group * GS + ((own_r >> 3) & 7) * CAP + rank
             slot_rows[pl.ds(field, 1), :] = slot.astype(F32)
 
-    slot_cols[...] = slot_rows[...].T.astype(jnp.int32)
-
-    @pl.loop(0, QUADS)
-    def _(quad):
-        back = lax.rem(128 - 4 * quad, 128)
-        ids = pltpu.roll(ids_ref[...], back, 1)
-        slots = pltpu.roll(slot_cols[...], back, 1)
-        total = jnp.zeros((NG, 128), F32)
-        for q in range(4):
-            tag = ((ids[:, q : q + 1] & (RQ - 1)) + 1).astype(F32)
-            place = (slots[:, q : q + 1] & (GS - 1)) + q * GS
-            right = jnp.where(iota((B, 128), 1) == place, tag, 0.0).astype(BF)
-            row = slot_rows[pl.ds(quad * 4 + q, 1), :].astype(jnp.int32)
-            left = jnp.where(iota((NG, B), 0) == (row >> 5), 1.0, 0.0).astype(BF)
-            total = total + jnp.dot(left, right, preferred_element_type=F32)
-        tag_send[pl.ds(quad, NG, stride=8), :] = total
-
-    tag_send[pl.ds(QUADS, NG, stride=8), :] = jnp.zeros((NG, 128), F32)
-    pl.semaphore_wait(barrier, NG + 1)
-
-    def rows8(g):
-        return pl.ds(pl.multiple_of(g * 8, 8), 8)
-
-    @pl.loop(1, NG)
-    def _(i):
-        g = lax.rem(me + i, NG)
-        pltpu.make_async_remote_copy(
-            src_ref=tag_send.at[rows8(g)], dst_ref=tag_recv.at[rows8(me)],
-            send_sem=tag_send_sem, recv_sem=tag_recv_sem, device_id=device_of(g, z), device_id_type=MESH,
-        ).start()
-
-    pltpu.make_async_copy(tag_send.at[rows8(me)], tag_recv.at[rows8(me)], tag_recv_sem).start()
-    load.wait()
-
     def place(chunk):
         @pl.loop(0, FC)
         def _(k):
@@ -150,10 +155,50 @@
                 send_sem=send_sem, recv_sem=recv_sem.at[chunk], device_id=device_of(g, z), device_id_type=MESH,
             ).start()
 
-    @pl.loop(0, AHEAD)
-    def _(chunk):
-        place(chunk)
-
+    pl.semaphore_wait(barrier, NG + 1)
+
+    @pl.loop(0, AHEAD * FC // 4)
+    def _(quad):
+        rank_quad(quad)
+
+        @pl.loop(0, 4 // FC)
+        def _(i):
+            place(quad * (4 // FC) + i)
+
+    @pl.loop(AHEAD * FC // 4, QUADS)
+    def _(quad):
+        rank_quad(quad)
+
+    slot_cols[...] = slot_rows[...].T.astype(jnp.int32)
+
+    @pl.loop(0, QUADS)
+    def _(quad):
+        back = lax.rem(128 - 4 * quad, 128)
+        ids = pltpu.roll(ids_cols[...], back, 1)
+        slots = pltpu.roll(slot_cols[...], back, 1)
+        total = jnp.zeros((NG, 128), F32)
+        for q in range(4):
+            tag = ((ids[:, q : q + 1] & (RQ - 1)) + 1).astype(F32)
+            place = (slots[:, q : q + 1] & (GS - 1)) + q * GS
+            right = jnp.where(iota((B, 128), 1) == place, tag, 0.0).astype(BF)
+            row = slot_rows[pl.ds(quad * 4 + q, 1), :].astype(jnp.int32)
+            group = jnp.where(iota((NG, B), 0) == (row >> 5), 1.0, 0.0).astype(BF)
+            total = total + jnp.dot(group, right, preferred_element_type=F32)
+        tag_send[pl.ds(quad, NG, stride=8), :] = total
+
+    tag_send[pl.ds(QUADS, NG, stride=8), :] = jnp.zeros((NG, 128), F32)
+    def rows8(g):
+        return pl.ds(pl.multiple_of(g * 8, 8), 8)
+
+    @pl.loop(1, NG)
+    def _(i):
+        g = lax.rem(me + i, NG)
+        pltpu.make_async_remote_copy(
+            src_ref=tag_send.at[rows8(g)], dst_ref=tag_recv.at[rows8(me)],
+            send_sem=tag_send_sem, recv_sem=tag_recv_sem, device_id=device_of(g, z), device_id_type=MESH,
+        ).start()
+
+    pltpu.make_async_copy(tag_send.at[rows8(me)], tag_recv.at[rows8(me)], tag_recv_sem).start()
     pltpu.make_async_copy(tag_recv, tag_recv, tag_recv_sem).wait()
     tags = tag_recv[...].astype(BF)
     for q in range(4):
@@ -217,8 +262,22 @@
         for k in range(FC):
             out_ref[chunk * FC + k] += both[k * RQ : (k + 1) * RQ]
 
-    @pl.loop(0, C + 4)
+    lag = (0, 2, 3, 4, 5)
+
+    @pl.loop(0, C + lag[4])
     def _(t):
+        for step in range(1, 4):
+
+            @pl.when((t >= lag[step]) & (t < C + lag[step]))
+            def _():
+                add(step, t - lag[step])
+
+        for step in range(1, 4):
+
+            @pl.when((t >= lag[step]) & (t < C + lag[step]))
+            def _():
+                forward(step, t - lag[step])
+
         @pl.when(t + AHEAD < C)
         def _():
             place(t + AHEAD)
@@ -226,22 +285,11 @@
         @pl.when(t < C)
         def _():
             tally(t)
-
-        for step in range(1, 4):
-
-            @pl.when((t >= step) & (t < C + step))
-            def _():
-                add(step, t - step)
-
-        @pl.when(t >= 4)
+            forward(0, t)
+
+        @pl.when(t >= lag[4])
         def _():
-            finish(t - 4)
-
-        for step in range(4):
-
-            @pl.when((t >= step) & (t < C + step))
-            def _():
-                forward(step, t - step)
+            finish(t - lag[4])
 
     sent = send.at[:, pl.ds(0, NG - 1)]
     pltpu.make_async_copy(sent, sent, send_sem).wait()
@@ -253,16 +301,23 @@
             pltpu.make_async_copy(ref, ref, ring_send_sem.at[d]).wait()
 
 
-def exchange(ids, ids_t, grads):
+def interact(ids_t, features, pair_grad, table):
     vmem = pl.BlockSpec(memory_space=pltpu.VMEM)
     dma = pltpu.SemaphoreType.DMA
     return pl.pallas_call(
         exchange_kernel,
-        out_shape=jax.ShapeDtypeStruct((F, RQ, E), F32),
-        in_specs=[vmem, vmem, pl.BlockSpec(memory_space=pl.ANY)],
-        out_specs=vmem,
+        out_shape=(jax.ShapeDtypeStruct((F, RQ, E), F32), jax.ShapeDtypeStruct((B, E), F32)),
+        in_specs=[vmem, pl.BlockSpec(memory_space=pl.ANY), vmem, vmem],
+        out_specs=(vmem, vmem),
         scratch_shapes=[
+            pltpu.VMEM((V, B, E), BF),
+            pltpu.VMEM((384, B), F32),
+            pltpu.VMEM((QUADS, B, 128), BF),
+            pltpu.VMEM((4, 128, 32 * SB), BF),
+            pltpu.VMEM((NB, 4 * QUADS * SB, 32 * SB), BF),
             pltpu.VMEM((F, B, E), BF),
+            pltpu.VMEM((128, B), F32),
+            pltpu.VMEM((B, 128), jnp.int32),
             pltpu.VMEM((128, B), F32),
             pltpu.VMEM((B, 128), jnp.int32),
             pltpu.VMEM((NG * 8, 128), F32),
@@ -276,24 +331,15 @@
             dma, dma, dma((C,)), dma, dma, dma((2,)), dma((2, 4, C)),
         ],
         compiler_params=pltpu.CompilerParams(
-            collective_id=0, has_side_effects=True, vmem_limit_bytes=60 * 2**20
+            collective_id=0, has_side_effects=True, vmem_limit_bytes=63 * 2**20
         ),
-        name="exchange",
-    )(ids, ids_t, grads)
+        name="interact",
+    )(ids_t, features, pair_grad, table)
 
 
 def local(sample_ids, features, pair_grad):
-    vectors = features.shape[1]
-    samples = features.shape[0]
-    spread = jnp.asarray(pair_table(vectors).T).astype(BF)
-    symmetric = jnp.dot(spread, pair_grad, preferred_element_type=F32)
-    symmetric = symmetric.astype(BF).reshape(vectors, vectors, samples)
-    gradients = jnp.einsum("fgb,bge->fbe", symmetric, features, preferred_element_type=F32)
-    dense_grad = gradients[0]
-    field_grads = gradients[1:].astype(BF)
-    ids = jnp.pad(sample_ids, ((0, 0), (0, 128 - F)))
-    ids_t = jnp.pad(sample_ids.T, ((0, 32 - F), (0, 0)))
-    return (exchange(ids, ids_t, field_grads), dense_grad)
+    table = jnp.asarray(pair_table()).astype(BF)
+    return interact(sample_ids.T, features.transpose(1, 0, 2), pair_grad, table)
 
 
 def solution(mesh):

time: 172 us -> 141 us (0.82)
  local copies, waits for them, and re-layouts: 28.4 us -> 3.56 us
  matrix products: 7.27 us -> 0 us
  Pallas kernels: 133 us -> 136 us
    reshape x2 -> x0, local copies, waits for them, and re-layouts: 9.73 us -> none  [local(): symmetric = symmetric.astype(BF).reshape(vectors, vectors, samples)]
    dot_general x2 -> x0, matrix products: 7.27 us -> none  [the longest x1 4.54 us: local(): jnp.einsum('fgb,bge->fbe', symmetric, features, preferred_element_type=F32)]
    dot_general x1 -> x0, local copies, waits for them, and re-layouts: 4.1 us -> none  [local(): jnp.einsum('fgb,bge->fbe', symmetric, features, preferred_element_type=F32)]
    unnamed x6 -> x4, local copies, waits for them, and re-layouts: 7.42 us -> 3.56 us
    pad x2 -> x0, local copies, waits for them, and re-layouts: 3.14 us -> none  [the longest x1 1.67 us: local(): ids = jnp.pad(sample_ids, ((0, 0), (0, 128 - F)))]
    pallas_call x1, Pallas kernels: 133 us -> 136 us  [interact(): pl.pallas_call(exchange_kernel, out_shape=(jax.ShapeDtypeStruct((F, RQ, E...]
    slice x1 -> x0, local copies, waits for them, and re-layouts: 2.35 us -> none  [local(): field_grads = gradients[1:].astype(BF)]
where the time goes in v2:
time: 141 us; the launch traced here: 140 us
  Pallas kernels  136 us (96%)
  local copies, waits for them, and re-layouts  3.56 us (3%)
    pallas_call x1, Pallas kernels, interact(): pl.pallas_call(exchange_kernel, out_shape=(jax.ShapeDtypeStruct((F, RQ, E...  136 us
    unnamed x4, local copies, waits for them, and re-layouts  3.56 us

profile of v2, /device:TPU:8, one launch (start us, length us, event | category | flops | bytes accessed | tf_op | source)
XLA Modules:
  0.0 140.0 jit_solution(3937189273514841335)
XLA Ops:
  0.6 135.8 %interact.1 = (f32[26,128,128]{2,1,0:T(8,128)}, f32[512,128]{1,0:T(8,128)}) custom-call(s32[26,512]{1,0:T(8,128)} %bitcast.3, bf16[27,512,128]{2,1,0:T(8,128)(2,1)} %bitcast.2, bf16[351,512]{1,0:T(8,128)(2,1)} %pairs_ref.1, bf16[384,896]{1,0:T(8,128)(2,1)} %constant.3.table_ref), custom_call_target="tpu_custom_call" | custom-call | tf_op jit(solution)/shard_map/interact/pallas_call | solution.py:307
  136.4 0.0 copy-start
  136.4 2.9 %copy.8 = f32[26,128,128]{2,1,0:T(8,128)} copy(f32[26,128,128]{2,1,0:T(8,128)} %get-tuple-element.4) | data formatting | bytes 3407872
  139.3 0.0 copy-done
  139.3 0.7 copy.9
Async XLA Ops:
  136.4 2.9 %copy-start = (f32[512,128]{1,0:T(8,128)S(1)}, f32[512,128]{1,0:T(8,128)}, u32[]{:S(2)}) copy-start(f32[512,128]{1,0:T(8,128)} %get-tuple-element.5) | copy-start | bytes 786436

commit v3 on v2

--- a/solution.py
+++ b/solution.py
@@ -28,7 +28,7 @@
 
 V = F + 1
 PAIRS = V * F // 2
-SB = 16
+SB = 8
 NB = B // SB
 
 
@@ -83,24 +83,33 @@
         ).astype(BF)
     for q in range(4):
         expand[q] = jnp.where(
-            iota((128, 32 * SB), 0) == q * 32 + (iota((128, 32 * SB), 1) >> 4), 1.0, 0.0
+            iota((128, 32 * SB), 0) == q * 32 + (iota((128, 32 * SB), 1) >> 3), 1.0, 0.0
         ).astype(BF)
 
     @pl.loop(0, QUADS)
     def _(quad):
-        @pl.loop(0, 4)
-        def _(q):
-            wide = jnp.dot(picked[quad], expand[q], preferred_element_type=F32).reshape(NB, SB, 32 * SB)
-            own = iota((1, SB, 32 * SB), 1) == (iota((1, SB, 32 * SB), 2) & (SB - 1))
-            left[:, pl.ds(pl.multiple_of((quad * 4 + q) * SB, SB), SB), :] = jnp.where(own, wide, 0.0).astype(BF)
+        own = iota((1, SB, 32 * SB), 1) == (iota((1, SB, 32 * SB), 2) & (SB - 1))
+        for pair in range(2):
+            both = [
+                jnp.dot(picked[quad], expand[pair * 2 + q], preferred_element_type=F32).reshape(NB, SB, 32 * SB)
+                for q in range(2)
+            ]
+            both = jnp.concatenate([jnp.where(own, wide, 0.0) for wide in both], axis=1)
+            left[:, pl.ds(pl.multiple_of((quad * 2 + pair) * 2 * SB, 2 * SB), 2 * SB), :] = both.astype(BF)
 
     load.wait()
 
-    @pl.loop(0, NB)
+    @pl.loop(0, NB // 2, unroll=4)
     def _(g):
-        at = pl.ds(pl.multiple_of(g * SB, SB), SB)
-        right = jnp.concatenate([feats[:, at, :], jnp.zeros((32 - V, SB, E), BF)], axis=0).reshape(32 * SB, E)
-        result = jnp.dot(left[g], right, preferred_element_type=F32).reshape(4 * QUADS, SB, E)
+        at = pl.ds(pl.multiple_of(g * 2 * SB, 2 * SB), 2 * SB)
+        wide = feats[:, at, :].astype(F32)
+        results = []
+        for h in range(2):
+            right = jnp.concatenate([wide[:, h * SB : (h + 1) * SB], jnp.zeros((32 - V, SB, E), F32)], axis=0)
+            right = right.reshape(32 * SB, E).astype(BF)
+            result = jnp.dot(left[g * 2 + h], right, preferred_element_type=F32)
+            results.append(result.reshape(4 * QUADS, SB, E))
+        result = jnp.concatenate(results, axis=1)
         dense_ref[at, :] = result[0]
         grads[:, at, :] = result[1:V].astype(BF)
 
@@ -262,22 +271,8 @@
         for k in range(FC):
             out_ref[chunk * FC + k] += both[k * RQ : (k + 1) * RQ]
 
-    lag = (0, 2, 3, 4, 5)
-
-    @pl.loop(0, C + lag[4])
+    @pl.loop(0, C + 4)
     def _(t):
-        for step in range(1, 4):
-
-            @pl.when((t >= lag[step]) & (t < C + lag[step]))
-            def _():
-                add(step, t - lag[step])
-
-        for step in range(1, 4):
-
-            @pl.when((t >= lag[step]) & (t < C + lag[step]))
-            def _():
-                forward(step, t - lag[step])
-
         @pl.when(t + AHEAD < C)
         def _():
             place(t + AHEAD)
@@ -287,9 +282,21 @@
             tally(t)
             forward(0, t)
 
-        @pl.when(t >= lag[4])
+        def ring_step(act, step):
+            @pl.when((t >= step) & (t < C + step))
+            def _():
+                act(step, t - step)
+
+        ring_step(add, 1)
+        ring_step(add, 2)
+        ring_step(forward, 1)
+        ring_step(add, 3)
+        ring_step(forward, 2)
+        ring_step(forward, 3)
+
+        @pl.when(t >= 4)
         def _():
-            finish(t - lag[4])
+            finish(t - 4)
 
     sent = send.at[:, pl.ds(0, NG - 1)]
     pltpu.make_async_copy(sent, sent, send_sem).wait()

time: 141 us -> 129 us (0.915)
  Pallas kernels: 136 us -> 125 us
    pallas_call x1, Pallas kernels: 136 us -> 125 us  [interact(): pl.pallas_call(exchange_kernel, out_shape=(jax.ShapeDtypeStruct((F, RQ, E...]
where the time goes in v3:
time: 129 us
  Pallas kernels  125 us (97%)
  local copies, waits for them, and re-layouts  3.56 us (3%)
    pallas_call x1, Pallas kernels, interact(): pl.pallas_call(exchange_kernel, out_shape=(jax.ShapeDtypeStruct((F, RQ, E...  125 us
    unnamed x4, local copies, waits for them, and re-layouts  3.56 us

profile of v3, /device:TPU:8, one launch (start us, length us, event | category | flops | bytes accessed | tf_op | source)
XLA Modules:
  0.0 128.7 jit_solution(16985521562030476983)
XLA Ops:
  0.6 124.5 %interact.1 = (f32[26,128,128]{2,1,0:T(8,128)}, f32[512,128]{1,0:T(8,128)}) custom-call(s32[26,512]{1,0:T(8,128)} %bitcast.3, bf16[27,512,128]{2,1,0:T(8,128)(2,1)} %bitcast.2, bf16[351,512]{1,0:T(8,128)(2,1)} %pairs_ref.1, bf16[384,896]{1,0:T(8,128)(2,1)} %constant.3.table_ref), custom_call_target="tpu_custom_call" | custom-call | tf_op jit(solution)/shard_map/interact/pallas_call | solution.py:314
  125.1 0.0 copy-start
  125.2 2.9 %copy.8 = f32[26,128,128]{2,1,0:T(8,128)} copy(f32[26,128,128]{2,1,0:T(8,128)} %get-tuple-element.4) | data formatting | bytes 3407872
  128.0 0.0 copy-done
  128.0 0.7 copy.9
Async XLA Ops:
  125.1 2.9 %copy-start = (f32[512,128]{1,0:T(8,128)S(1)}, f32[512,128]{1,0:T(8,128)}, u32[]{:S(2)}) copy-start(f32[512,128]{1,0:T(8,128)} %get-tuple-element.5) | copy-start | bytes 786436

commit v4 on v3

--- a/solution.py
+++ b/solution.py
@@ -141,7 +141,7 @@
             slot_rows[pl.ds(field, 1), :] = slot.astype(F32)
 
     def place(chunk):
-        @pl.loop(0, FC)
+        @pl.loop(0, FC, unroll=2)
         def _(k):
             field = chunk * FC + k
             row = slot_rows[pl.ds(field, 1), :].astype(jnp.int32)
@@ -222,7 +222,7 @@
     def tally(chunk):
         pltpu.make_async_copy(recv.at[chunk], recv.at[chunk], recv_sem.at[chunk]).wait()
 
-        @pl.loop(0, FC)
+        @pl.loop(0, FC, unroll=2)
         def _(k):
             field = chunk * FC + k
             want = wanted[field % 4, pl.ds(field // 4, 1), :]

time: 129 us -> 128 us (level)
  no operation moved by 1% of the time
where the time goes in v4:
time: 128 us
  Pallas kernels  124 us (97%)
  local copies, waits for them, and re-layouts  3.56 us (3%)
    pallas_call x1, Pallas kernels, interact(): pl.pallas_call(exchange_kernel, out_shape=(jax.ShapeDtypeStruct((F, RQ, E...  124 us
    unnamed x4, local copies, waits for them, and re-layouts  3.56 us

profile of v4, /device:TPU:8, one launch (start us, length us, event | category | flops | bytes accessed | tf_op | source)
XLA Modules:
  0.0 127.9 jit_solution(10347746703266138020)
XLA Ops:
  0.6 123.7 %interact.1 = (f32[26,128,128]{2,1,0:T(8,128)}, f32[512,128]{1,0:T(8,128)}) custom-call(s32[26,512]{1,0:T(8,128)} %bitcast.3, bf16[27,512,128]{2,1,0:T(8,128)(2,1)} %bitcast.2, bf16[351,512]{1,0:T(8,128)(2,1)} %pairs_ref.1, bf16[384,896]{1,0:T(8,128)(2,1)} %constant.3.table_ref), custom_call_target="tpu_custom_call" | custom-call | tf_op jit(solution)/shard_map/interact/pallas_call | solution.py:314
  124.3 0.0 copy-start
  124.3 2.9 %copy.8 = f32[26,128,128]{2,1,0:T(8,128)} copy(f32[26,128,128]{2,1,0:T(8,128)} %get-tuple-element.4) | data formatting | bytes 3407872
  127.2 0.0 copy-done
  127.2 0.7 copy.9
Async XLA Ops:
  124.3 2.9 %copy-start = (f32[512,128]{1,0:T(8,128)S(1)}, f32[512,128]{1,0:T(8,128)}, u32[]{:S(2)}) copy-start(f32[512,128]{1,0:T(8,128)} %get-tuple-element.5) | copy-start | bytes 786436
